TPU v7x, 32 devices: a whole 2x2x4 slice. The times are simulated.
32 devices in a mesh: parts: 2 (over y), blk: 4 (over z), grp: 4 (over x, core).
Axes of the slice: x: 2, y: 2, z: 4, core: 2. Of those that a mesh axis runs over, the one named last changes fastest.
Arguments:
- factors: float32 [64, 4096], P(None, ('parts', 'blk', 'grp')), parts along dimension 1, may hold values from -1 to 1
- tangent: float32 [64, 4096], P(None, ('parts', 'blk', 'grp')), parts along dimension 1, may hold values from -15 to 15
- counts: int32 [4096, 2048], P(('parts', 'blk', 'grp')), parts along dimension 0, may hold values from 0 to 4, as said below
Outputs:
- hess_vec: float32 [64, 4096], P(None, ('parts', 'blk', 'grp')), parts along dimension 1
- residual: float32 [64, 4096], P(None, ('parts', 'blk', 'grp')), parts along dimension 1
- inner: float32 [4], P('parts'), parts along dimension 0
There are 2 independent parts, one for each index of `parts`. A program takes and returns all parts, laid end to end along the dimension named above; each array names one. Nothing has to cross between parts.
Inputs may be any that keep to these rules, and one draw needn't show every extreme that they name: counts is symmetric.
All inputs are finite; a program needn't handle non-finite values.
Results may differ from a plain program's by a relative error of at most 0.0003.
Values sent between devices are 32-bit elements; how exact they have to be, the bound alone decides.
A program may use at most 128 MiB of HBM per device.

v0:
```python
import jax
import jax.numpy as jnp
from jax import lax
from jax.sharding import PartitionSpec as P


def local(factors, tangent, counts):
    rows = counts.shape[0]
    nodes = counts.shape[1]
    scale = 1.0 / jnp.sqrt(jnp.float32(nodes))
    highest = lax.Precision.HIGHEST
    contract = (((0,), (0,)), ((), ()))
    right = (((1,), (1,)), ((), ()))
    row_start = (lax.axis_index("blk") * lax.axis_size("grp") + lax.axis_index("grp")) * rows
    row_ids = row_start + jnp.arange(rows, dtype=jnp.int32)[:, None]
    group_u, group_v = (
        lax.all_gather(factors, "grp", axis=1, tiled=True),
        lax.all_gather(tangent, "grp", axis=1, tiled=True),
    )
    piece_u = lax.all_gather(group_u, "blk", axis=1, tiled=True)
    piece_v = lax.all_gather(group_v, "blk", axis=1, tiled=True)
    width = piece_u.shape[1]
    eta = lax.dot_general(factors, piece_u, contract, precision=highest)
    deta = lax.dot_general(factors, piece_v, contract, precision=highest) + lax.dot_general(
        tangent, piece_u, contract, precision=highest
    )
    col_ids = jnp.arange(width, dtype=jnp.int32)[None, :]
    keep = row_ids != col_ids
    rate = jnp.where(keep, jnp.exp(eta), jnp.float32(0.0))
    weight = rate * deta
    tile_counts = counts.astype(jnp.float32)
    slack = jnp.where(keep, tile_counts - rate, jnp.float32(0.0))
    hess_acc = lax.dot_general(piece_u, weight, right, precision=highest)
    resid_acc = lax.dot_general(piece_u, slack - weight, right, precision=highest)
    hess_acc, resid_acc = (hess_acc, resid_acc)
    hess_vec = hess_acc * scale
    residual = resid_acc * scale
    sum_sq, sum_curv = lax.psum(
        (jnp.sum(residual * residual), jnp.sum(tangent * hess_vec)), ("blk", "grp")
    )
    inner = jnp.stack([sum_sq, sum_curv])
    return (hess_vec, residual, inner)


def solution(mesh):
    return jax.shard_map(
        local,
        mesh=mesh,
        in_specs=(
            P(None, ("parts", "blk", "grp")),
            P(None, ("parts", "blk", "grp")),
            P(("parts", "blk", "grp"), None),
        ),
        out_specs=(P(None, ("parts", "blk", "grp")), P(None, ("parts", "blk", "grp")), P("parts")),
        check_vma=False,
    )
```

profile of v0, /device:TPU:0, one launch (start us, length us, event | category | flops | bytes accessed | tf_op | source)
XLA Modules:
  0.0 85.9 jit_solution(17943244656120877728)
XLA Ops:
  0.6 0.0 copy-start.1
  0.7 6.7 %all_gather.12 = f32[64,512]{1,0:T(8,128)S(1)} all-gather(f32[64,128]{1,0:T(8,128)} %param.3), channel_id=1, replica_groups=mesh['parts'=2,'blk'=4,'grp'=4] {'grp'}, dimensions={1}, use_global_device_ids=true | all-gather | bytes 163840 | tf_op jit(solution)/shard_map/all_gather | solution.py:17
  7.4 0.0 copy-done.1
  7.4 5.6 %all_gather.14 = f32[64,512]{1,0:T(8,128)S(1)} all-gather(f32[64,128]{1,0:T(8,128)S(1)} %copy-done.1), channel_id=1, replica_groups=mesh['parts'=2,'blk'=4,'grp'=4] {'grp'}, dimensions={1}, use_global_device_ids=true | all-gather | bytes 163840 | tf_op jit(solution)/shard_map/all_gather | solution.py:18
  12.9 16.6 %all_gather.13 = f32[64,2048]{1,0:T(8,128)S(1)} all-gather(f32[64,512]{1,0:T(8,128)S(1)} %all_gather.12), channel_id=1, replica_groups=mesh['parts'=2,'blk'=4,'grp'=4] {'blk'}, dimensions={1}, use_global_device_ids=true | all-gather | bytes 655360 | tf_op jit(solution)/shard_map/all_gather | solution.py:20
  29.5 0.0 copy-start.2
  29.5 16.0 %all_gather.15 = f32[64,2048]{1,0:T(8,128)S(1)} all-gather(f32[64,512]{1,0:T(8,128)S(1)} %all_gather.14), channel_id=1, replica_groups=mesh['parts'=2,'blk'=4,'grp'=4] {'blk'}, dimensions={1}, use_global_device_ids=true | all-gather | bytes 655360 | tf_op jit(solution)/shard_map/all_gather | solution.py:21
  45.5 0.0 copy-done.2
  45.5 1.0 %fusion.11 = f32[128,2048]{1,0:T(8,128)S(1)} fusion(f32[64,128]{1,0:T(8,128)S(1)} %copy-done.2, f32[64,2048]{1,0:T(8,128)S(1)} %all_gather.15), kind=kOutput, calls=%fused_computation.20 | convolution fusion | flops 201326592 | bytes 1605632 | tf_op jit(solution)/shard_map/dot_general | solution.py:24
  46.6 1.1 %fusion.1 = f32[128,2048]{1,0:T(8,128)S(1)} fusion(f32[64,128]{1,0:T(8,128)S(1)} %copy-done.2, f32[64,2048]{1,0:T(8,128)S(1)} %all_gather.13, s32[128]{0:T(128)S(1)} %iota_add_fusion), kind=kOutput, calls=%fused_computation.3 | convolution fusion | flops 201850880 | bytes 1606144 | tf_op jit(solution)/shard_map/dot_general | solution.py:23
  47.7 0.0 copy-start
  47.7 1.1 %fusion = f32[128,2048]{1,0:T(8,128)S(1)} fusion(f32[128,2048]{1,0:T(8,128)S(1)} %fusion.1, f32[128,2048]{1,0:T(8,128)S(1)} %fusion.11, f32[64,128]{1,0:T(8,128)S(1)} %copy-done.1, f32[64,2048]{1,0:T(8,128)S(1)} %all_gather.13), kind=kOutput, calls=%fused_computation.1 | convolution fusion | flops 201850880 | bytes 3702784 | tf_op jit(solution)/shard_map/dot_general | solution.py:24
  48.8 0.2 copy-done
  48.9 2.7 %multiply_reduce_fusion.1 = (f32[]{:T(128)}, f32[64,128]{1,0:T(8,128)}) fusion(f32[64,2048]{1,0:T(8,128)S(1)} %all_gather.13, f32[128,2048]{1,0:T(8,128)S(1)} %fusion, f32[128,2048]{1,0:T(8,128)S(1)} %fusion.1, s32[128,2048]{1,0:T(8,128)S(1)} %copy-done, s32[128]{0:T(128)S(1)} %iota_add_fusion), kind=kOutput, calls=%fused_computation.16 | convolution fusion | flops 202661888 | bytes 3703300 | tf_op jit(solution)/shard_map/dot_general | solution.py:34
  51.6 2.4 %multiply_reduce_fusion = (f32[]{:T(128)}, f32[64,128]{1,0:T(8,128)}) fusion(f32[64,128]{1,0:T(8,128)S(1)} %copy-done.1, f32[128,2048]{1,0:T(8,128)S(1)} %fusion, f32[64,2048]{1,0:T(8,128)S(1)} %all_gather.13), kind=kOutput, calls=%fused_computation.15 | convolution fusion | flops 201351168 | bytes 1638404 | tf_op jit(solution)/shard_map/dot_general | solution.py:33
  54.0 30.1 %all-reduce = (f32[1]{0:T(128)}, f32[1]{0:T(128)}) all-reduce(f32[1]{0:T(128)} %bitcast.3, f32[1]{0:T(128)} %bitcast.2), channel_id=1, replica_groups=mesh['parts'=2,'blk'=4,'grp'=4] {'blk','grp'}, use_global_device_ids=true, to_apply=%region_3.4 | all-reduce | flops 2 | bytes 16 | tf_op jit(solution)/shard_map/psum | solution.py:38
  84.2 1.8 %pad_maximum_fusion = f32[2]{0:T(128)} fusion(f32[1]{0:T(128)} %get-tuple-element.3, f32[1]{0:T(128)} %get-tuple-element.4), kind=kLoop, calls=%fused_computation.17 | loop fusion | flops 2 | bytes 16 | tf_op jit(solution)/shard_map/stack | solution.py:41
  (1 shorter events, 0.0 us)
Async XLA Ops:
  0.6 6.7 %copy-start.1 = (f32[64,128]{1,0:T(8,128)S(1)}, f32[64,128]{1,0:T(8,128)}, u32[]{:S(2)}) copy-start(f32[64,128]{1,0:T(8,128)} %param.4) | copy-start | bytes 98308
  29.5 16.0 %copy-start.2 = (f32[64,128]{1,0:T(8,128)S(1)}, f32[64,128]{1,0:T(8,128)}, u32[]{:S(2)}) copy-start(f32[64,128]{1,0:T(8,128)} %param.3) | copy-start | bytes 98308
  47.7 1.2 %copy-start = (s32[128,2048]{1,0:T(8,128)S(1)}, s32[128,2048]{1,0:T(8,128)}, u32[]{:S(2)}) copy-start(s32[128,2048]{1,0:T(8,128)} %param.5) | copy-start | bytes 3145732
where the time goes:
time: 86.3 us; the launch traced here: 85.9 us
  blocking collectives  75 us (87%)
  matrix products  8.3 us (10%)
  other arithmetic  1.78 us (2%)
    psum x1, blocking collectives, local(): lax.psum((jnp.sum(residual * residual), jnp.sum(tangent * hess_vec)), ('b...  30.1 us
    all_gather x1, blocking collectives, local(): piece_u = lax.all_gather(group_u, 'blk', axis=1, tiled=True)  16.6 us
    all_gather x1, blocking collectives, local(): piece_v = lax.all_gather(group_v, 'blk', axis=1, tiled=True)  16 us
    all_gather x1, blocking collectives, local(): lax.all_gather(factors, 'grp', axis=1, tiled=True)  6.69 us
    all_gather x1, blocking collectives, local(): lax.all_gather(tangent, 'grp', axis=1, tiled=True)  5.58 us
    dot_general x1, matrix products, local(): lax.dot_general(piece_u, slack - weight, right, precision=highest)  2.69 us
    dot_general x1, matrix products, local(): hess_acc = lax.dot_general(piece_u, weight, right, precision=highest)  2.41 us
    another operation x1, other arithmetic, local(): inner = jnp.stack([sum_sq, sum_curv])  1.78 us

commit v1 on v0

--- a/solution.py
+++ b/solution.py
@@ -17,8 +17,11 @@
         lax.all_gather(factors, "grp", axis=1, tiled=True),
         lax.all_gather(tangent, "grp", axis=1, tiled=True),
     )
-    piece_u = lax.all_gather(group_u, "blk", axis=1, tiled=True)
-    piece_v = lax.all_gather(group_v, "blk", axis=1, tiled=True)
+    piece_u, piece_v = jnp.split(
+        lax.all_gather(jnp.concatenate([group_u, group_v], axis=0), "blk", axis=1, tiled=True),
+        [group_u.shape[0]],
+        axis=0,
+    )
     width = piece_u.shape[1]
     eta = lax.dot_general(factors, piece_u, contract, precision=highest)
     deta = lax.dot_general(factors, piece_v, contract, precision=highest) + lax.dot_general(

time: 86.3 us -> 102 us (1.18)
  blocking collectives: 75 us -> 45 us
  waiting for transfers between devices: 0 us -> 29.2 us
  between operations: 0.69 us -> 14.1 us
  matrix products: 8.3 us -> 10.7 us
    all_gather x2 -> x0, blocking collectives: 32.6 us -> none  [the longest x1 16.6 us: local(): piece_u = lax.all_gather(group_u, 'blk', axis=1, tiled=True)]
    all_gather x0 -> x1, waiting for transfers between devices: none -> 29.2 us  [local(): lax.all_gather(jnp.concatenate([group_u, group_v], axis=0), 'blk', axis=1...]
    psum x1, blocking collectives: 30.1 us -> 32.6 us  [local(): lax.psum((jnp.sum(residual * residual), jnp.sum(tangent * hess_vec)), ('b...]
    dot_general x1, matrix products: 1.03 us -> 2.94 us  [local(): lax.dot_general(factors, piece_v, contract, precision=highest)]
    all_gather x1, blocking collectives: 5.58 us -> 6.82 us  [local(): lax.all_gather(tangent, 'grp', axis=1, tiled=True)]
    all_gather x1, blocking collectives: 6.69 us -> 5.58 us  [local(): lax.all_gather(factors, 'grp', axis=1, tiled=True)]
  transfers between devices with their start and end apart: 0 -> 1, of which waited for: 0 -> 1; matrix products, arithmetic and copies ran while one was open for 0% -> 0% of each run, Pallas kernels for 0% -> 0%
where the time goes in v1:
time: 102 us
  blocking collectives  45 us (44%)
  waiting for transfers between devices  29.2 us (29%)
  between operations  14.1 us (14%)
  matrix products  10.7 us (10%)
  other arithmetic  2.56 us (3%)
    psum x1, blocking collectives, local(): lax.psum((jnp.sum(residual * residual), jnp.sum(tangent * hess_vec)), ('b...  32.6 us
    all_gather x1, waiting for transfers between devices, local(): lax.all_gather(jnp.concatenate([group_u, group_v], axis=0), 'blk', axis=1...  29.2 us
    all_gather x1, blocking collectives, local(): lax.all_gather(tangent, 'grp', axis=1, tiled=True)  6.82 us
    all_gather x1, blocking collectives, local(): lax.all_gather(factors, 'grp', axis=1, tiled=True)  5.58 us
    dot_general x1, matrix products, local(): lax.dot_general(factors, piece_v, contract, precision=highest)  2.94 us
    dot_general x1, matrix products, local(): lax.dot_general(piece_u, slack - weight, right, precision=highest)  2.19 us
  transfers between devices with their start and end apart: 1, of which 1 were waited for; matrix products, arithmetic and copies ran while one was open for 0% of the time, Pallas kernels for 0%

profile of v1, /device:TPU:0, one launch (start us, length us, event | category | flops | bytes accessed | tf_op | source)
XLA Modules:
  0.0 102.0 jit_solution(14580952171395302995)
XLA Ops:
  7.2 0.0 copy-start.3
  7.2 0.0 copy-start.1
  7.2 0.0 all-gather.2.cloned.1.call-start
  7.2 6.8 %all_gather.10 = f32[64,512]{1,0:T(8,128)S(1)} all-gather(f32[64,128]{1,0:T(8,128)} %param.4), channel_id=1, replica_groups=mesh['parts'=2,'blk'=4,'grp'=4] {'grp'}, dimensions={1}, use_global_device_ids=true | all-gather | bytes 163840 | tf_op jit(solution)/shard_map/all_gather | solution.py:18
  14.1 0.0 copy-done.3
  14.1 5.6 %all_gather.9 = f32[64,512]{1,0:T(8,128)S(1)} all-gather(f32[64,128]{1,0:T(8,128)S(1)} %copy-done.3), channel_id=1, replica_groups=mesh['parts'=2,'blk'=4,'grp'=4] {'grp'}, dimensions={1}, use_global_device_ids=true | all-gather | bytes 163840 | tf_op jit(solution)/shard_map/all_gather | solution.py:17
  19.6 0.7 pad_maximum_fusion
  20.4 0.0 all-gather.2.cloned.1.call-update
  20.4 0.0 copy-done.1
  20.4 0.3 copy.6
  20.8 29.2 %all-gather.2.cloned.1.call-done = f32[128,2048]{1,0:T(8,128)} async-done(((f32[128,512]{1,0:T(8,128)}), f32[128,2048]{1,0:T(8,128)}) %all-gather.2.cloned.1.call-update) | async-done | bytes 1048592 | tf_op jit(solution)/shard_map/all_gather | solution.py:21
  50.0 0.0 copy-start
  50.0 2.9 %fusion.8 = f32[2048,128]{1,0:T(8,128)S(1)} fusion(f32[64,128]{1,0:T(8,128)S(1)} %copy-done.3, f32[128,2048]{1,0:T(8,128)} %all-gather.2.cloned.1.call-done), kind=kOutput, calls=%fused_computation.13 | convolution fusion | flops 201326592 | bytes 1605632 | tf_op jit(solution)/shard_map/dot_general | solution.py:27
  52.9 0.0 copy-done
  52.9 0.0 copy-start.2
  53.0 1.8 %fusion.3 = f32[128,2048]{0,1:T(8,128)S(1)} fusion(f32[64,128]{1,0:T(8,128)S(1)} %copy-done.3, s32[128]{0:T(128)S(1)} %iota_add_fusion, f32[128,2048]{1,0:T(8,128)S(1)} %copy-done), kind=kOutput, calls=%fused_computation.5 | convolution fusion | flops 201850880 | bytes 1606144 | tf_op jit(solution)/shard_map/dot_general | solution.py:26
  54.8 0.0 copy-done.2
  54.8 1.8 %fusion.1 = f32[128,2048]{0,1:T(8,128)S(1)} fusion(f32[128,2048]{0,1:T(8,128)S(1)} %fusion.3, f32[2048,128]{1,0:T(8,128)S(1)} %fusion.8, f32[64,128]{1,0:T(8,128)S(1)} %copy-done.2, f32[128,2048]{1,0:T(8,128)S(1)} %copy-done), kind=kOutput, calls=%fused_computation.2 | convolution fusion | flops 201850880 | bytes 3702784 | tf_op jit(solution)/shard_map/dot_general | solution.py:27
  56.6 2.0 %multiply_reduce_fusion = (f32[]{:T(128)}, f32[64,128]{1,0:T(8,128)}) fusion(f32[64,128]{1,0:T(8,128)S(1)} %copy-done.2, f32[128,2048]{0,1:T(8,128)S(1)} %fusion.1, f32[128,2048]{1,0:T(8,128)S(1)} %copy-done), kind=kOutput, calls=%fused_computation.22 | convolution fusion | flops 201351168 | bytes 1638404 | tf_op jit(solution)/shard_map/dot_general | solution.py:36
  58.6 2.2 %multiply_reduce_fusion.1 = (f32[]{:T(128)}, f32[64,128]{1,0:T(8,128)}) fusion(f32[128,2048]{0,1:T(8,128)S(1)} %fusion.1, f32[128,2048]{0,1:T(8,128)S(1)} %fusion.3, s32[128,2048]{0,1:T(8,128)S(1)} %copy.6, s32[128]{0:T(128)S(1)} %iota_add_fusion, f32[128,2048]{1,0:T(8,128)S(1)} %copy-done), kind=kOutput, calls=%fused_computation.23 | convolution fusion | flops 202661888 | bytes 3703300 | tf_op jit(solution)/shard_map/dot_general | solution.py:37
  60.7 32.6 %all-reduce = (f32[1]{0:T(128)}, f32[1]{0:T(128)}) all-reduce(f32[1]{0:T(128)} %bitcast.3, f32[1]{0:T(128)} %bitcast.2), channel_id=1, replica_groups=mesh['parts'=2,'blk'=4,'grp'=4] {'blk','grp'}, use_global_device_ids=true, to_apply=%region_3.4 | all-reduce | flops 2 | bytes 16 | tf_op jit(solution)/shard_map/psum | solution.py:41
  93.3 1.8 %pad_maximum_fusion.1 = f32[2]{0:T(128)} fusion(f32[1]{0:T(128)} %get-tuple-element.3, f32[1]{0:T(128)} %get-tuple-element.4), kind=kLoop, calls=%fused_computation.24 | loop fusion | flops 2 | bytes 16 | tf_op jit(solution)/shard_map/stack | solution.py:44
  (1 shorter events, 0.0 us)
Async XLA Ops:
  7.2 6.9 %copy-start.3 = (f32[64,128]{1,0:T(8,128)S(1)}, f32[64,128]{1,0:T(8,128)}, u32[]{:S(2)}) copy-start(f32[64,128]{1,0:T(8,128)} %param.3) | copy-start | bytes 98308
  7.2 13.2 %copy-start.1 = (s32[128,2048]{1,0:T(8,128)S(1)}, s32[128,2048]{1,0:T(8,128)}, u32[]{:S(2)}) copy-start(s32[128,2048]{1,0:T(8,128)} %param.5) | copy-start | bytes 3145732
  7.2 42.8 %all-gather.2.cloned.1.call-start = ((), (), s32[]{:S(2)}) async-start(), calls=%async_computation | async-start | bytes 1310720 | tf_op jit(solution)/shard_map/all_gather | solution.py:21
  50.0 3.0 %copy-start = (f32[128,2048]{1,0:T(8,128)S(1)}, f32[128,2048]{1,0:T(8,128)}, u32[]{:S(2)}) copy-start(f32[128,2048]{1,0:T(8,128)} %all-gather.2.cloned.1.call-done) | copy-start | bytes 3145732
  52.9 1.8 %copy-start.2 = (f32[64,128]{1,0:T(8,128)S(1)}, f32[64,128]{1,0:T(8,128)}, u32[]{:S(2)}) copy-start(f32[64,128]{1,0:T(8,128)} %param.4) | copy-start | bytes 98308
Sparse Core Ops, SparseCore 0:
  20.5 29.4 all-gather.1
